TPU v7x, 256 devices: a whole 4x4x8 slice. The times are simulated.
256 devices in a mesh: dp: 64 (over y, z_hi, x), mp: 4 (over z_lo, core).
Axes of the slice: x: 4, y: 4, z: 8 (z_hi: 4, z_lo: 2; z = z_hi * 2 + z_lo), core: 2. Of those that a mesh axis runs over, the one named last changes fastest.
Arguments:
- tokens: bfloat16 [4096, 2, 3072], P('dp'), may hold values from -6 to 6
- norm_gain_vector: float32 [3072], replicated, may hold values from 0.5 to 1.5
- query_weight: bfloat16 [3072, 1536], P('dp', 'mp'), may hold values from -0.109375 to 0.109375
- key_weight: bfloat16 [3072, 1536], P('dp', 'mp'), may hold values from -0.4375 to 0.4375
- value_weight: bfloat16 [3072, 1536], P('dp', 'mp'), may hold values from -0.109375 to 0.109375
- output_weight: bfloat16 [3072, 1536], P('dp', 'mp'), may hold values from -0.15625 to 0.15625
- prefix_cache: bfloat16 [64, 64, 2, 1536], P('dp', None, None, 'mp'), may hold values from -64 to 64
- lengths: int32 [4096], P('dp'), may hold values from 1 to 2, 5120 in all
- groups: int32 [4096], P('dp'), may hold values from 0 to 3
- deal_slot: int32 [4096], P('dp'), may hold values from 0 to 4095, as said below
- owners: int32 [64], replicated, may hold values from 0 to 63, each once
Outputs:
- hidden: bfloat16 [4096, 2, 3072], P('dp', None, 'mp')
- suffix_cache: bfloat16 [4096, 2, 2, 1536], P('dp', None, None, 'mp')
Inputs may be any that keep to these rules, and one draw needn't show every extreme that they name: Every value once; the 64 requests that start on one index of dp go to 64 different devices deal_slot // 64, one to each.
All inputs are finite; a program needn't handle non-finite values. No bound on the sum of `lengths` on one device may be relied on, other than what follows from the above.
Results may differ from a plain program's by a relative error of at most 0.013.
The roundings to bfloat16 on the way count: a program that leaves them out, or rounds other values in their place, can miss the bound.
Values may be sent and summed in bfloat16 or wider, within the bound.
No kernel may reach another device: no remote copies, remote signals or barrier semaphores. Data moves between devices by JAX's collectives and lax.ppermute only.
A program may use at most 128 MiB of HBM per device.

v0:
```python
import math
import jax
import jax.numpy as jnp
from jax import lax
from jax.sharding import PartitionSpec as P

HD = 96
GROUPS = 4
PBLK = 64
NEG_FILL = -1e30


def rope_tables(slot_len, head_dim, first_pos):
    position = (first_pos + jnp.arange(slot_len)).astype(jnp.float32)
    frequency = 10000.0 ** (-jnp.arange(head_dim // 2).astype(jnp.float32) * 2.0 / head_dim)
    angles = position[:, None] * frequency[None, :]
    angles = jnp.concatenate([angles, angles], axis=-1)
    return (jnp.cos(angles)[:, None, :], jnp.sin(angles)[:, None, :])


def rope_rotate(values, cosine, sine_table):
    half_dim = values.shape[-1] // 2
    turned = jnp.concatenate([-values[..., half_dim:], values[..., :half_dim]], axis=-1)
    return values * cosine + turned * sine_table


def project(tokens, norm_gain_vector, query_weight, key_weight, value_weight, prefix_len):
    requests, slot_len, model_width = tokens.shape
    widened_rows = tokens.astype(jnp.float32)
    reciprocal_root_scale = lax.rsqrt(
        jnp.mean(widened_rows * widened_rows, axis=-1, keepdims=True) + 1e-05
    )
    normalized_rows = (
        (widened_rows * reciprocal_root_scale * norm_gain_vector)
        .astype(jnp.bfloat16)
        .reshape(requests * slot_len, model_width)
    )
    head_cols = query_weight.shape[1]
    pieces = (
        lax.all_gather(query_weight, "dp", axis=0, tiled=True),
        lax.all_gather(key_weight, "dp", axis=0, tiled=True),
        lax.all_gather(value_weight, "dp", axis=0, tiled=True),
    )
    queries, keyed, valued = tuple(
        (
            jnp.dot(normalized_rows, weight_rows, preferred_element_type=jnp.float32)
            for weight_rows in pieces
        )
    )
    heads_local = head_cols // HD
    cosine, sine_table = rope_tables(slot_len, HD, prefix_len)

    def shaped(values):
        return values.reshape(requests, slot_len, heads_local, HD)

    queries = (
        rope_rotate(shaped(queries), cosine, sine_table)
        .astype(jnp.bfloat16)
        .reshape(requests, slot_len, head_cols)
    )
    keyed = (
        rope_rotate(shaped(keyed), cosine, sine_table)
        .astype(jnp.bfloat16)
        .reshape(requests, slot_len, head_cols)
    )
    valued = valued.astype(jnp.bfloat16).reshape(requests, slot_len, head_cols)
    return jnp.concatenate([queries, keyed, valued], axis=-1)


def attend(packed, length_in, group_in, prefix_cache, owners):
    requests, slot_len, triple = packed.shape
    head_cols = triple // 3
    heads_local = head_cols // HD
    row_count = requests * slot_len
    devices = lax.axis_size("dp")
    blocks_per = devices // GROUPS
    inv_scale = 1.0 / math.sqrt(HD)
    queries = packed[..., :head_cols].reshape(requests, slot_len, heads_local, HD)
    keyed = packed[..., head_cols : 2 * head_cols].reshape(requests, slot_len, heads_local, HD)
    valued = packed[..., 2 * head_cols :].reshape(requests, slot_len, heads_local, HD)
    position = jnp.arange(slot_len)
    allowed = (position[None, :, None] >= position[None, None, :]) & (
        position[None, None, :] < length_in[:, None, None]
    )
    allowed = allowed[:, None]
    self_scores = (
        jnp.einsum("rthd,rshd->rhts", queries, keyed, preferred_element_type=jnp.float32)
        * inv_scale
    )
    self_max = jnp.max(jnp.where(allowed, self_scores, NEG_FILL), axis=-1)
    self_weights = jnp.where(allowed, jnp.exp(self_scores - self_max[..., None]), 0.0)
    self_sum = jnp.sum(self_weights, axis=-1)
    self_acc = jnp.einsum(
        "rhts,rshd->rhtd",
        self_weights.astype(jnp.bfloat16),
        valued,
        preferred_element_type=jnp.float32,
    )
    run_max = jnp.transpose(self_max, (1, 0, 2)).reshape(heads_local, row_count)
    run_sum = jnp.transpose(self_sum, (1, 0, 2)).reshape(heads_local, row_count)
    run_acc = jnp.transpose(self_acc, (1, 0, 2, 3)).reshape(heads_local, row_count, HD)
    flat_queries = queries.reshape(row_count, heads_local, HD)
    query_group = jnp.repeat(group_in, slot_len)
    slot_ids = jnp.arange(devices, dtype=jnp.int32)
    owner_match = owners[None, :] == slot_ids[:, None]
    slot_group = jnp.sum(jnp.where(owner_match, (slot_ids // blocks_per)[None, :], 0), axis=1)
    shard_rows = lax.all_gather(prefix_cache, "dp", axis=0, tiled=True)
    slot_count = shard_rows.shape[0]
    block_len = shard_rows.shape[1]
    key_count = slot_count * block_len
    key_rows = shard_rows[:, :, 0].reshape(key_count, heads_local, HD)
    value_rows = shard_rows[:, :, 1].reshape(key_count, heads_local, HD)
    key_slot = jnp.arange(key_count, dtype=jnp.int32) // block_len
    key_group = jnp.sum(
        jnp.where(key_slot[:, None] == slot_ids[None, :], slot_group[None, :], 0), axis=1
    )
    key_block = math.gcd(key_count, 512)

    def absorb_block(carry_state, block_index):
        prior_max, prior_sum, prior_acc = carry_state
        keys_of_block = lax.dynamic_slice_in_dim(key_rows, block_index * key_block, key_block, 0)
        block_values = lax.dynamic_slice_in_dim(value_rows, block_index * key_block, key_block, 0)
        block_group = lax.dynamic_slice_in_dim(key_group, block_index * key_block, key_block, 0)
        scores = (
            jnp.einsum(
                "qhd,khd->hqk", flat_queries, keys_of_block, preferred_element_type=jnp.float32
            )
            * inv_scale
        )
        matched = (query_group[:, None] == block_group[None, :])[None]
        block_max = jnp.max(jnp.where(matched, scores, NEG_FILL), axis=-1)
        new_max = jnp.maximum(prior_max, block_max)
        weights = jnp.where(matched, jnp.exp(scores - new_max[..., None]), 0.0)
        shrink = jnp.exp(prior_max - new_max)
        new_sum = prior_sum * shrink + jnp.sum(weights, axis=-1)
        new_acc = prior_acc * shrink[..., None] + jnp.einsum(
            "hqk,khd->hqd",
            weights.astype(jnp.bfloat16),
            block_values,
            preferred_element_type=jnp.float32,
        )
        return ((new_max, new_sum, new_acc), None)

    carry_out, _ = lax.scan(
        absorb_block, (run_max, run_sum, run_acc), jnp.arange(key_count // key_block)
    )
    run_max, run_sum, run_acc = carry_out
    attended = (run_acc / run_sum[..., None]).astype(jnp.bfloat16)
    attended = jnp.transpose(attended, (1, 0, 2)).reshape(requests, slot_len, head_cols)
    live_mask = position[None, :] < length_in[:, None]
    stacked_parts = jnp.stack(
        [packed[..., head_cols : 2 * head_cols], packed[..., 2 * head_cols :]], axis=2
    )
    stacked_parts = jnp.where(
        live_mask[:, :, None, None], stacked_parts, jnp.zeros_like(stacked_parts)
    )
    return (attended, stacked_parts)


def on_device(
    tokens,
    norm_gain_vector,
    query_weight,
    key_weight,
    value_weight,
    output_weight,
    prefix_cache,
    lengths,
    groups,
    deal_slot,
    owners,
):
    requests, slot_len, model_width = tokens.shape
    devices = lax.axis_size("dp")
    head_cols = query_weight.shape[1]
    prefix_len = PBLK * devices // GROUPS
    dest_device = deal_slot // requests
    send_order = jnp.argsort(dest_device)
    restore = jnp.argsort(send_order)
    request_info = jnp.stack([deal_slot, lengths, groups], axis=1)
    moved_rows, info_in = (
        lax.all_to_all(tokens[send_order], "dp", split_axis=0, concat_axis=0, tiled=True),
        lax.all_to_all(request_info[send_order], "dp", split_axis=0, concat_axis=0, tiled=True),
    )
    packed = project(
        moved_rows, norm_gain_vector, query_weight, key_weight, value_weight, prefix_len
    )
    attended, stacked_parts = attend(packed, info_in[:, 1], info_in[:, 2], prefix_cache, owners)
    suffix_cache = stacked_parts[jnp.argsort(info_in[:, 0] % requests)]
    attended_home = lax.all_to_all(attended, "dp", split_axis=0, concat_axis=0, tiled=True)[restore]
    flat_attended = attended_home.reshape(requests * slot_len, head_cols)
    partial_terms = lax.dot_general(
        flat_attended,
        lax.all_gather(output_weight, "dp", axis=0, tiled=True),
        (((1,), (1,)), ((), ())),
        preferred_element_type=jnp.float32,
    )
    summed = lax.psum_scatter(
        partial_terms.astype(jnp.bfloat16), "mp", scatter_dimension=1, tiled=True
    ).astype(jnp.float32)
    live_mask = (jnp.arange(slot_len)[None, :] < lengths[:, None]).reshape(requests * slot_len, 1)
    hidden = (
        jnp.where(live_mask, summed, 0.0)
        .astype(jnp.bfloat16)
        .reshape(requests, slot_len, summed.shape[1])
    )
    return (hidden, suffix_cache)


def solution(mesh):
    in_specs = (
        P("dp", None, None),
        P(),
        P("dp", "mp"),
        P("dp", "mp"),
        P("dp", "mp"),
        P("dp", "mp"),
        P("dp", None, None, "mp"),
        P("dp"),
        P("dp"),
        P("dp"),
        P(),
    )
    out_specs = (P("dp", None, "mp"), P("dp", None, None, "mp"))
    return jax.shard_map(
        on_device, mesh=mesh, in_specs=in_specs, out_specs=out_specs, check_vma=False
    )
```

profile of v0, /device:TPU:1, one launch (start us, length us, event | category | flops | bytes accessed | tf_op | source)
XLA Modules:
  0.0 492.5 jit_solution(8548728937993800416)
XLA Ops:
  9.5 1.5 copy.158
  12.5 2.0 sort.45
  14.6 1.2 gather_fusion
  15.7 15.1 %all-to-all-start = ((s32[64,1,3]{2,1,0:T(1,128)}), s32[64,1,3]{2,1,0:T(1,128)S(1)}, u32[]{:S(2)}, u32[]{:S(2)}) async-start(s32[64,1,3]{2,1,0:T(1,128)} %bitcast.4), calls=%async_computation | async-start | bytes 65536 | tf_op jit(solution)/shard_map/all_to_all | solution.py:183
  31.5 3.0 gather_fusion.1
  34.5 2.1 sort.46
  36.6 5.1 %all-to-all-done = s32[64,1,3]{2,1,0:T(1,128)S(1)} async-done(((s32[64,1,3]{2,1,0:T(1,128)}), s32[64,1,3]{2,1,0:T(1,128)S(1)}, u32[]{:S(2)}, u32[]{:S(2)}) %all-to-all-start) | async-done | bytes 800 | tf_op jit(solution)/shard_map/all_to_all | solution.py:183
  41.6 7.3 %all-to-all-start.1 = ((bf16[64,2,3072]{2,1,0:T(2,128)(2,1)}), bf16[64,2,3072]{2,1,0:T(2,128)(2,1)S(1)}, u32[]{:S(2)}, u32[]{:S(2)}) async-start(bf16[64,2,3072]{2,1,0:T(2,128)(2,1)} %gather_fusion.1), calls=%async_computation.1 | async-start | bytes 1572864 | tf_op jit(solution)/shard_map/all_to_all | solution.py:182
  50.0 22.7 %all-to-all-done.1 = bf16[64,2,3072]{2,1,0:T(2,128)(2,1)S(1)} async-done(((bf16[64,2,3072]{2,1,0:T(2,128)(2,1)}), bf16[64,2,3072]{2,1,0:T(2,128)(2,1)S(1)}, u32[]{:S(2)}, u32[]{:S(2)}) %all-to-all-start.1) | async-done | bytes 786464 | tf_op jit(solution)/shard_map/all_to_all | solution.py:182
  73.6 0.9 fusion.16
  75.8 22.8 %all-gather.6.cloned.1.call-done = bf16[3072,384]{1,0:T(8,128)(2,1)} async-done(((bf16[48,384]{1,0:T(8,128)(2,1)}), bf16[3072,384]{1,0:T(8,128)(2,1)}) %all-gather.6.cloned.1.call-update) | async-done | bytes 2359312 | tf_op jit(solution)/shard_map/all_gather | solution.py:40
  98.7 4.3 copy.143
  102.9 76.2 %all-gather.8.cloned.1.call-done = bf16[3072,384]{1,0:T(8,128)(2,1)} async-done(((bf16[48,384]{1,0:T(8,128)(2,1)}), bf16[3072,384]{1,0:T(8,128)(2,1)}) %all-gather.8.cloned.1.call-update) | async-done | bytes 2359312 | tf_op jit(solution)/shard_map/all_gather | solution.py:41
  179.2 4.3 copy.145
  183.5 2.9 fusion.19
  186.4 1.1 fusion.17
  188.8 70.9 %all-gather.10.cloned.1.call-done = bf16[3072,384]{1,0:T(8,128)(2,1)} async-done(((bf16[48,384]{1,0:T(8,128)(2,1)}), bf16[3072,384]{1,0:T(8,128)(2,1)}) %all-gather.10.cloned.1.call-update) | async-done | bytes 2359312 | tf_op jit(solution)/shard_map/all_gather | solution.py:42
  259.7 2.2 convolution_convert_fusion.1
  263.2 98.9 %all-gather.12.cloned.1.call-done = bf16[64,64,2,384]{3,1,2,0:T(8,128)(2,1)} async-done(((bf16[1,64,2,384]{3,1,2,0:T(8,128)(2,1)}), bf16[64,64,2,384]{3,1,2,0:T(8,128)(2,1)}) %all-gather.12.cloned.1.call-update) | async-done | bytes 6291472 | tf_op jit(solution)/shard_map/all_gather | solution.py:107
  362.1 6.2 %fusion.38 = (bf16[64,64,1,384]{3,1,2,0:T(8,128)(2,1)}, bf16[64,64,1,384]{3,1,2,0:T(8,128)(2,1)}) fusion(bf16[64,64,2,384]{3,1,2,0:T(8,128)(2,1)} %all-gather.12.cloned.1.call-done), kind=kLoop, calls=%fused_computation.99 | loop fusion | bytes 12582912 | tf_op jit(solution)/shard_map/slice | solution.py:112
  368.4 8.8 %reshape_squeeze.6 = bf16[4096,4,96]{2,1,0:T(4,128)(2,1)} reshape(bf16[64,64,1,384]{3,1,2,0:T(8,128)(2,1)} %get-tuple-element.164) | data formatting | bytes 6291456 | tf_op jit(solution)/shard_map/reshape;squeeze | solution.py:111
  377.2 7.3 %copy.163 = bf16[4096,4,96]{0,2,1:T(8,128)(2,1)} copy(bf16[4096,4,96]{2,1,0:T(4,128)(2,1)} %reshape_squeeze.6) | data formatting | bytes 6291456
  384.5 8.8 %reshape_squeeze.7 = bf16[4096,4,96]{2,1,0:T(4,128)(2,1)} reshape(bf16[64,64,1,384]{3,1,2,0:T(8,128)(2,1)} %get-tuple-element.163) | data formatting | bytes 6291456 | tf_op jit(solution)/shard_map/reshape;squeeze | solution.py:112
  393.3 7.3 %copy.165 = bf16[4096,4,96]{0,2,1:T(8,128)(2,1)} copy(bf16[4096,4,96]{2,1,0:T(4,128)(2,1)} %reshape_squeeze.7) | data formatting | bytes 6291456
  400.6 37.5 %while.15 = (s32[]{:T(128)}, f32[4,128]{1,0:T(4,128)S(1)}, f32[4,128]{1,0:T(4,128)S(1)}, f32[4,128,96]{1,2,0:T(8,128)S(1)}, s32[8]{0:T(128)S(1)}, /*index=5*/s32...) while((s32[]{:T(128)}, f32[4,128]{1,0:T(4,128)S(1)}, ...), condition=%wide.region_9.10_spmd.clone, body=%wide.region_6.9_spmd.clone.sunk | while | flops 103187456 | bytes 4727243 | solution.py:144
  402.3 1.4 select_reduce_fusion.5
  403.9 1.4 convolution_add_fusion.2
  407.0 1.4 select_reduce_fusion.5
  408.6 1.4 convolution_add_fusion.2
  411.7 1.4 select_reduce_fusion.5
  413.3 1.4 convolution_add_fusion.2
  416.4 1.4 select_reduce_fusion.5
  418.0 1.4 convolution_add_fusion.2
  421.1 1.4 select_reduce_fusion.5
  422.7 1.3 convolution_add_fusion.2
  425.8 1.4 select_reduce_fusion.5
  427.4 1.4 convolution_add_fusion.2
  430.4 1.4 select_reduce_fusion.5
  432.1 1.3 convolution_add_fusion.2
  435.2 1.4 select_reduce_fusion.5
  436.8 1.4 convolution_add_fusion.2
  439.2 11.7 %all-to-all-start.2 = ((bf16[64,2,384]{2,1,0:T(2,128)(2,1)}), bf16[64,2,384]{2,1,0:T(2,128)(2,1)S(1)}, u32[]{:S(2)}, u32[]{:S(2)}) async-start(bf16[64,2,384]{2,1,0:T(2,128)(2,1)} %reshape.253), calls=%async_computation.2 | async-start | bytes 196608 | tf_op jit(solution)/shard_map/all_to_all | solution.py:190
  451.1 11.1 %all-to-all-done.2 = bf16[64,2,384]{2,1,0:T(2,128)(2,1)S(1)} async-done(((bf16[64,2,384]{2,1,0:T(2,128)(2,1)}), bf16[64,2,384]{2,1,0:T(2,128)(2,1)S(1)}, u32[]{:S(2)}, u32[]{:S(2)}) %all-to-all-start.2) | async-done | bytes 98336 | tf_op jit(solution)/shard_map/all_to_all | solution.py:190
  463.1 3.4 convolution_convert_fusion
  466.8 2.0 sort.47
  469.7 1.7 gather_fusion.3
  471.4 12.5 %reduce-scatter.2.cloned.1.call-done = bf16[128,768]{1,0:T(8,128)(2,1)} async-done(((bf16[128,3072]{1,0:T(8,128)(2,1)}), bf16[128,768]{1,0:T(8,128)(2,1)}) %reduce-scatter.2.cloned.1.call-update) | async-done | bytes 196624 | tf_op jit(solution)/shard_map/reduce_scatter | solution.py:198
  483.9 1.0 select_convert_fusion
  (155 shorter events, 23.8 us)
Async XLA Ops:
  7.2 24.3 %copy-start = (bf16[64,2,3072]{2,1,0:T(2,128)(2,1)S(1)}, bf16[64,2,3072]{2,1,0:T(2,128)(2,1)}, u32[]{:S(2)}) copy-start(bf16[64,2,3072]{2,1,0:T(2,128)(2,1)} %param.13) | copy-start | bytes 2359300
  7.2 42.0 %copy-start.4 = (s32[64]{0:T(128)S(1)}, s32[64]{0:T(128)}, u32[]{:S(2)}) copy-start(s32[64]{0:T(128)} %param.23) | copy-start | bytes 772
  7.2 91.5 %all-gather.6.cloned.1.call-start = ((), (), s32[]{:S(2)}) async-start(), calls=%async_computation.4 | async-start | bytes 2396160 | tf_op jit(solution)/shard_map/all_gather | solution.py:40
  7.9 171.3 %all-gather.8.cloned.1.call-start = ((), (), s32[]{:S(2)}) async-start(), calls=%async_computation.5 | async-start | bytes 2396160 | tf_op jit(solution)/shard_map/all_gather | solution.py:41
  8.7 251.0 %all-gather.10.cloned.1.call-start = ((), (), s32[]{:S(2)}) async-start(), calls=%async_computation.6 | async-start | bytes 2396160 | tf_op jit(solution)/shard_map/all_gather | solution.py:42
  9.4 352.7 %all-gather.12.cloned.1.call-start = ((), (), s32[]{:S(2)}) async-start(), calls=%async_computation.7 | async-start | bytes 6389760 | tf_op jit(solution)/shard_map/all_gather | solution.py:107
  11.0 62.6 %copy-start.2 = (f32[3072]{0:T(1024)S(1)}, f32[3072]{0:T(1024)}, u32[]{:S(2)}) copy-start(f32[3072]{0:T(1024)} %param.14) | copy-start | bytes 36868
  15.7 25.9 %all-to-all-start = ((s32[64,1,3]{2,1,0:T(1,128)}), s32[64,1,3]{2,1,0:T(1,128)S(1)}, u32[]{:S(2)}, u32[]{:S(2)}) async-start(s32[64,1,3]{2,1,0:T(1,128)} %bitcast.4), calls=%async_computation | async-start | bytes 65536 | tf_op jit(solution)/shard_map/all_to_all | solution.py:183
  30.9 432.2 %all-gather.14.cloned.1.call-start = ((), (), s32[]{:S(2)}) async-start(), calls=%async_computation.8 | async-start | bytes 2396160 | tf_op jit(solution)/shard_map/all_gather | solution.py:194
  41.6 31.1 %all-to-all-start.1 = ((bf16[64,2,3072]{2,1,0:T(2,128)(2,1)}), bf16[64,2,3072]{2,1,0:T(2,128)(2,1)S(1)}, u32[]{:S(2)}, u32[]{:S(2)}) async-start(bf16[64,2,3072]{2,1,0:T(2,128)(2,1)} %gather_fusion.1), calls=%async_computation.1 | async-start | bytes 1572864 | tf_op jit(solution)/shard_map/all_to_all | solution.py:182
  183.5 2.9 copy-start.1
  439.2 27.3 %copy-start.3 = (s32[64]{0:T(128)S(1)}, s32[64]{0:T(128)}, u32[]{:S(2)}) copy-start(s32[64]{0:T(128)} %param.20) | copy-start | bytes 772
  439.2 23.0 %all-to-all-start.2 = ((bf16[64,2,384]{2,1,0:T(2,128)(2,1)}), bf16[64,2,384]{2,1,0:T(2,128)(2,1)S(1)}, u32[]{:S(2)}, u32[]{:S(2)}) async-start(bf16[64,2,384]{2,1,0:T(2,128)(2,1)} %reshape.253), calls=%async_computation.2 | async-start | bytes 196608 | tf_op jit(solution)/shard_map/all_to_all | solution.py:190
  451.0 32.9 %reduce-scatter.2.cloned.1.call-start = ((), (), s32[]{:S(2)}) async-start(), calls=%async_computation.9 | async-start | bytes 983040 | tf_op jit(solution)/shard_map/reduce_scatter | solution.py:198
Sparse Core Ops, SparseCore 0:
  11.2 87.4 all-gather.5
  101.8 77.2 all-gather.7
  182.4 77.2 all-gather.9
  263.4 98.6 all-gather.11
  365.2 77.9 all-gather.13
  466.6 17.2 reduce-scatter.1
where the time goes:
time: 494 us; the launch traced here: 493 us
  waiting for transfers between devices  323 us (65%)
  local copies, waits for them, and re-layouts  66.6 us (13%)
  starting transfers between devices  34.4 us (7%)
  matrix products  32.3 us (7%)
  other arithmetic  16.1 us (3%)
  between operations  14.5 us (3%)
  loops' own time  5.66 us (1%)
    all_gather x1, waiting for transfers between devices, attend(): shard_rows = lax.all_gather(prefix_cache, 'dp', axis=0, tiled=True)  98.9 us
    all_gather x1, waiting for transfers between devices, project(): lax.all_gather(key_weight, 'dp', axis=0, tiled=True)  76.2 us
    all_gather x1, waiting for transfers between devices, project(): lax.all_gather(value_weight, 'dp', axis=0, tiled=True)  70.9 us
    all_gather x1, waiting for transfers between devices, project(): lax.all_gather(query_weight, 'dp', axis=0, tiled=True)  22.8 us
    all_to_all x1, waiting for transfers between devices, on_device(): lax.all_to_all(tokens[send_order], 'dp', split_axis=0, concat_axis=0, til...  22.7 us
    unnamed x17, local copies, waits for them, and re-layouts  16.5 us
    all_to_all x1, starting transfers between devices, on_device(): lax.all_to_all(request_info[send_order], 'dp', split_axis=0, concat_axis=...  15.1 us
    reduce_scatter x1, waiting for transfers between devices, on_device(): lax.psum_scatter(partial_terms.astype(jnp.bfloat16), 'mp', scatter_dimens...  12.5 us
  transfers between devices with their start and end apart: 9, of which 8 were waited for; matrix products, arithmetic and copies ran while one was open for 22% of the time, Pallas kernels for 0%

commit v1 on v0

--- a/solution.py
+++ b/solution.py
@@ -104,7 +104,8 @@
     slot_ids = jnp.arange(devices, dtype=jnp.int32)
     owner_match = owners[None, :] == slot_ids[:, None]
     slot_group = jnp.sum(jnp.where(owner_match, (slot_ids // blocks_per)[None, :], 0), axis=1)
-    shard_rows = lax.all_gather(prefix_cache, "dp", axis=0, tiled=True)
+    sent = jnp.stack([prefix_cache] * lax.axis_size("dp"))
+    shard_rows = jnp.concatenate(lax.all_to_all(sent, "dp", 0, 0), axis=0)
     slot_count = shard_rows.shape[0]
     block_len = shard_rows.shape[1]
     key_count = slot_count * block_len

time: 494 us -> 476 us (0.964)
  waiting for transfers between devices: 323 us -> 297 us
  starting transfers between devices: 34.4 us -> 39.5 us
    all_gather x1 -> x0, waiting for transfers between devices: 98.9 us -> none  [attend(): shard_rows = lax.all_gather(prefix_cache, 'dp', axis=0, tiled=True)]
    all_gather x1, waiting for transfers between devices: 76.2 us -> 135 us  [project(): lax.all_gather(key_weight, 'dp', axis=0, tiled=True)]
    all_gather x1, waiting for transfers between devices: 22.8 us -> 33.4 us  [project(): lax.all_gather(query_weight, 'dp', axis=0, tiled=True)]
    all_to_all x0 -> x1, starting transfers between devices: none -> 9.75 us  [attend(): shard_rows = jnp.concatenate(lax.all_to_all(sent, 'dp', 0, 0), axis=0)]
    unnamed x17 -> x18, local copies, waits for them, and re-layouts: 16.5 us -> 14.9 us
  transfers between devices with their start and end apart: 9 -> 9, of which waited for: 8 -> 7; matrix products, arithmetic and copies ran while one was open for 22% -> 24% of each run, Pallas kernels for 0% -> 0%
where the time goes in v1:
time: 476 us; the launch traced here: 474 us
  waiting for transfers between devices  297 us (62%)
  local copies, waits for them, and re-layouts  68.6 us (14%)
  starting transfers between devices  39.5 us (8%)
  matrix products  32.4 us (7%)
  other arithmetic  16.1 us (3%)
  between operations  14.2 us (3%)
  loops' own time  5.67 us (1%)
    all_gather x1, waiting for transfers between devices, project(): lax.all_gather(key_weight, 'dp', axis=0, tiled=True)  135 us
    all_gather x1, waiting for transfers between devices, project(): lax.all_gather(value_weight, 'dp', axis=0, tiled=True)  70.9 us
    all_gather x1, waiting for transfers between devices, project(): lax.all_gather(query_weight, 'dp', axis=0, tiled=True)  33.4 us
    all_to_all x1, waiting for transfers between devices, on_device(): lax.all_to_all(tokens[send_order], 'dp', split_axis=0, concat_axis=0, til...  22.9 us
    all_to_all x1, starting transfers between devices, on_device(): lax.all_to_all(request_info[send_order], 'dp', split_axis=0, concat_axis=...  15.1 us
    unnamed x18, local copies, waits for them, and re-layouts  14.9 us
    reduce_scatter x1, waiting for transfers between devices, on_device(): lax.psum_scatter(partial_terms.astype(jnp.bfloat16), 'mp', scatter_dimens...  14.1 us
    dot_general x8, matrix products, absorb_block(): jnp.einsum('qhd,khd->hqk', flat_queries, keys_of_block, preferred_element...  11.1 us
  transfers between devices with their start and end apart: 9, of which 7 were waited for; matrix products, arithmetic and copies ran while one was open for 24% of the time, Pallas kernels for 0%

profile of v1, /device:TPU:1, one launch (start us, length us, event | category | flops | bytes accessed | tf_op | source)
XLA Modules:
  0.0 473.8 jit_solution(16097703909207399091)
XLA Ops:
  10.1 2.0 sort.45
  12.2 1.2 gather_fusion
  13.4 15.1 %all-to-all-start = ((s32[64,1,3]{2,1,0:T(1,128)}), s32[64,1,3]{2,1,0:T(1,128)S(1)}, u32[]{:S(2)}, u32[]{:S(2)}) async-start(s32[64,1,3]{2,1,0:T(1,128)} %bitcast.4), calls=%async_computation | async-start | bytes 65536 | tf_op jit(solution)/shard_map/all_to_all | solution.py:184
  28.5 3.0 gather_fusion.1
  31.5 7.8 %all-to-all-done = s32[64,1,3]{2,1,0:T(1,128)S(1)} async-done(((s32[64,1,3]{2,1,0:T(1,128)}), s32[64,1,3]{2,1,0:T(1,128)S(1)}, u32[]{:S(2)}, u32[]{:S(2)}) %all-to-all-start) | async-done | bytes 800 | tf_op jit(solution)/shard_map/all_to_all | solution.py:184
  39.2 4.6 all-to-all-start.1
  43.9 22.9 %all-to-all-done.1 = bf16[64,2,3072]{2,1,0:T(2,128)(2,1)S(1)} async-done(((bf16[64,2,3072]{2,1,0:T(2,128)(2,1)}), bf16[64,2,3072]{2,1,0:T(2,128)(2,1)S(1)}, u32[]{:S(2)}, u32[]{:S(2)}) %all-to-all-start.1) | async-done | bytes 786464 | tf_op jit(solution)/shard_map/all_to_all | solution.py:183
  66.8 3.7 stack.13
  70.5 9.7 %all-to-all-start.2 = ((bf16[64,1,64,2,384]{4,2,3,1,0:T(8,128)(2,1)}), bf16[64,1,64,2,384]{4,2,3,1,0:T(8,128)(2,1)}, u32[]{:S(2)}, u32[]{:S(2)}) async-start(bf16[64,1,64,2,384]{4,2,3,1,0:T(8,128)(2,1)} %stack.13), calls=%async_computation.2 | async-start | bytes 12582912 | tf_op jit(solution)/shard_map/all_to_all | solution.py:108
  81.6 2.0 sort.46
  85.6 0.9 fusion.16
  87.8 33.4 %all-gather.5.cloned.1.call-done = bf16[3072,384]{1,0:T(8,128)(2,1)} async-done(((bf16[48,384]{1,0:T(8,128)(2,1)}), bf16[3072,384]{1,0:T(8,128)(2,1)}) %all-gather.5.cloned.1.call-update) | async-done | bytes 2359312 | tf_op jit(solution)/shard_map/all_gather | solution.py:40
  121.2 4.3 copy.143
  125.5 134.7 %all-gather.7.cloned.1.call-done = bf16[3072,384]{1,0:T(8,128)(2,1)} async-done(((bf16[48,384]{1,0:T(8,128)(2,1)}), bf16[3072,384]{1,0:T(8,128)(2,1)}) %all-gather.7.cloned.1.call-update) | async-done | bytes 2359312 | tf_op jit(solution)/shard_map/all_gather | solution.py:41
  260.2 4.3 copy.145
  264.5 2.9 fusion.19
  267.4 1.1 fusion.17
  269.9 70.9 %all-gather.9.cloned.1.call-done = bf16[3072,384]{1,0:T(8,128)(2,1)} async-done(((bf16[48,384]{1,0:T(8,128)(2,1)}), bf16[3072,384]{1,0:T(8,128)(2,1)}) %all-gather.9.cloned.1.call-update) | async-done | bytes 2359312 | tf_op jit(solution)/shard_map/all_gather | solution.py:42
  340.8 2.2 convolution_convert_fusion.1
  344.3 6.2 %fusion.38 = (bf16[64,64,1,384]{3,1,2,0:T(8,128)(2,1)}, bf16[64,64,1,384]{3,1,2,0:T(8,128)(2,1)}) fusion(bf16[64,64,2,384]{3,1,2,0:T(8,128)(2,1)} %bitcast.21), kind=kLoop, calls=%fused_computation.99 | loop fusion | bytes 12582912 | tf_op jit(solution)/shard_map/slice | solution.py:113
  350.5 8.8 %reshape_squeeze.6 = bf16[4096,4,96]{2,1,0:T(4,128)(2,1)} reshape(bf16[64,64,1,384]{3,1,2,0:T(8,128)(2,1)} %get-tuple-element.164) | data formatting | bytes 6291456 | tf_op jit(solution)/shard_map/reshape;squeeze | solution.py:112
  359.4 7.2 %copy.163 = bf16[4096,4,96]{0,2,1:T(8,128)(2,1)} copy(bf16[4096,4,96]{2,1,0:T(4,128)(2,1)} %reshape_squeeze.6) | data formatting | bytes 6291456
  366.6 8.8 %reshape_squeeze.7 = bf16[4096,4,96]{2,1,0:T(4,128)(2,1)} reshape(bf16[64,64,1,384]{3,1,2,0:T(8,128)(2,1)} %get-tuple-element.163) | data formatting | bytes 6291456 | tf_op jit(solution)/shard_map/reshape;squeeze | solution.py:113
  375.4 7.3 %copy.165 = bf16[4096,4,96]{0,2,1:T(8,128)(2,1)} copy(bf16[4096,4,96]{2,1,0:T(4,128)(2,1)} %reshape_squeeze.7) | data formatting | bytes 6291456
  382.7 37.6 %while.15 = (s32[]{:T(128)}, f32[4,128]{1,0:T(4,128)S(1)}, f32[4,128]{1,0:T(4,128)S(1)}, f32[4,128,96]{1,2,0:T(8,128)S(1)}, s32[8]{0:T(128)S(1)}, /*index=5*/s32...) while((s32[]{:T(128)}, f32[4,128]{1,0:T(4,128)S(1)}, ...), condition=%wide.region_9.10_spmd.clone, body=%wide.region_6.9_spmd.clone.sunk | while | flops 103187456 | bytes 4727243 | solution.py:145
  384.4 1.4 select_reduce_fusion.5
  386.0 1.4 convolution_add_fusion.2
  389.0 1.4 select_reduce_fusion.5
  390.7 1.4 convolution_add_fusion.2
  393.7 1.4 select_reduce_fusion.5
  395.4 1.3 convolution_add_fusion.2
  398.4 1.4 select_reduce_fusion.5
  400.0 1.4 convolution_add_fusion.2
  403.1 1.5 select_reduce_fusion.5
  404.8 1.4 convolution_add_fusion.2
  407.9 1.4 select_reduce_fusion.5
  409.5 1.4 convolution_add_fusion.2
  412.6 1.4 select_reduce_fusion.5
  414.2 1.4 convolution_add_fusion.2
  417.3 1.4 select_reduce_fusion.5
  418.9 1.4 convolution_add_fusion.2
  421.4 9.6 %all-to-all-start.3 = ((bf16[64,2,384]{2,1,0:T(2,128)(2,1)}), bf16[64,2,384]{2,1,0:T(2,128)(2,1)S(1)}, u32[]{:S(2)}, u32[]{:S(2)}) async-start(bf16[64,2,384]{2,1,0:T(2,128)(2,1)} %reshape.260), calls=%async_computation.3 | async-start | bytes 196608 | tf_op jit(solution)/shard_map/all_to_all | solution.py:191
  431.3 10.9 %all-to-all-done.3 = bf16[64,2,384]{2,1,0:T(2,128)(2,1)S(1)} async-done(((bf16[64,2,384]{2,1,0:T(2,128)(2,1)}), bf16[64,2,384]{2,1,0:T(2,128)(2,1)S(1)}, u32[]{:S(2)}, u32[]{:S(2)}) %all-to-all-start.3) | async-done | bytes 98336 | tf_op jit(solution)/shard_map/all_to_all | solution.py:191
  443.1 3.4 convolution_convert_fusion
  446.8 2.0 sort.47
  449.7 1.7 gather_fusion.3
  451.3 14.1 %reduce-scatter.2.cloned.1.call-done = bf16[128,768]{1,0:T(8,128)(2,1)} async-done(((bf16[128,3072]{1,0:T(8,128)(2,1)}), bf16[128,768]{1,0:T(8,128)(2,1)}) %reduce-scatter.2.cloned.1.call-update) | async-done | bytes 196624 | tf_op jit(solution)/shard_map/reduce_scatter | solution.py:199
  465.5 1.0 select_convert_fusion
  (157 shorter events, 24.0 us)
Async XLA Ops:
  7.2 21.3 %copy-start = (bf16[64,2,3072]{2,1,0:T(2,128)(2,1)S(1)}, bf16[64,2,3072]{2,1,0:T(2,128)(2,1)}, u32[]{:S(2)}) copy-start(bf16[64,2,3072]{2,1,0:T(2,128)(2,1)} %param.13) | copy-start | bytes 2359300
  7.2 36.7 %copy-start.2 = (bf16[1,64,2,384]{3,2,1,0:T(2,128)(2,1)S(1)}, bf16[1,64,2,384]{3,2,1,0:T(2,128)(2,1)}, u32[]{:S(2)}) copy-start(bf16[1,64,2,384]{3,2,1,0:T(2,128)(2,1)} %param.19) | copy-start | bytes 294916
  7.2 114.0 %all-gather.5.cloned.1.call-start = ((), (), s32[]{:S(2)}) async-start(), calls=%async_computation.5 | async-start | bytes 2396160 | tf_op jit(solution)/shard_map/all_gather | solution.py:40
  7.9 252.3 %all-gather.7.cloned.1.call-start = ((), (), s32[]{:S(2)}) async-start(), calls=%async_computation.6 | async-start | bytes 2396160 | tf_op jit(solution)/shard_map/all_gather | solution.py:41
  13.4 25.9 %all-to-all-start = ((s32[64,1,3]{2,1,0:T(1,128)}), s32[64,1,3]{2,1,0:T(1,128)S(1)}, u32[]{:S(2)}, u32[]{:S(2)}) async-start(s32[64,1,3]{2,1,0:T(1,128)} %bitcast.4), calls=%async_computation | async-start | bytes 65536 | tf_op jit(solution)/shard_map/all_to_all | solution.py:184
  39.2 27.5 %all-to-all-start.1 = ((bf16[64,2,3072]{2,1,0:T(2,128)(2,1)}), bf16[64,2,3072]{2,1,0:T(2,128)(2,1)S(1)}, u32[]{:S(2)}, u32[]{:S(2)}) async-start(bf16[64,2,3072]{2,1,0:T(2,128)(2,1)} %gather_fusion.1), calls=%async_computation.1 | async-start | bytes 1572864 | tf_op jit(solution)/shard_map/all_to_all | solution.py:183
  70.5 13.4 %copy-start.5 = (s32[64]{0:T(128)S(1)}, s32[64]{0:T(128)}, u32[]{:S(2)}) copy-start(s32[64]{0:T(128)} %param.23) | copy-start | bytes 772
  70.5 15.1 %copy-start.3 = (f32[3072]{0:T(1024)S(1)}, f32[3072]{0:T(1024)}, u32[]{:S(2)}) copy-start(f32[3072]{0:T(1024)} %param.14) | copy-start | bytes 36868
  70.5 273.8 %all-to-all-start.2 = ((bf16[64,1,64,2,384]{4,2,3,1,0:T(8,128)(2,1)}), bf16[64,1,64,2,384]{4,2,3,1,0:T(8,128)(2,1)}, u32[]{:S(2)}, u32[]{:S(2)}) async-start(bf16[64,1,64,2,384]{4,2,3,1,0:T(8,128)(2,1)} %stack.13), calls=%async_computation.2 | async-start | bytes 12582912 | tf_op jit(solution)/shard_map/all_to_all | solution.py:108
  80.2 260.5 %all-gather.9.cloned.1.call-start = ((), (), s32[]{:S(2)}) async-start(), calls=%async_computation.7 | async-start | bytes 2396160 | tf_op jit(solution)/shard_map/all_gather | solution.py:42
  81.0 362.1 %all-gather.11.cloned.1.call-start = ((), (), s32[]{:S(2)}) async-start(), calls=%async_computation.8 | async-start | bytes 2396160 | tf_op jit(solution)/shard_map/all_gather | solution.py:195
  264.5 2.9 copy-start.1
  421.4 25.1 %copy-start.4 = (s32[64]{0:T(128)S(1)}, s32[64]{0:T(128)}, u32[]{:S(2)}) copy-start(s32[64]{0:T(128)} %param.20) | copy-start | bytes 772
  421.4 20.8 %all-to-all-start.3 = ((bf16[64,2,384]{2,1,0:T(2,128)(2,1)}), bf16[64,2,384]{2,1,0:T(2,128)(2,1)S(1)}, u32[]{:S(2)}, u32[]{:S(2)}) async-start(bf16[64,2,384]{2,1,0:T(2,128)(2,1)} %reshape.260), calls=%async_computation.3 | async-start | bytes 196608 | tf_op jit(solution)/shard_map/all_to_all | solution.py:191
  431.0 34.5 %reduce-scatter.2.cloned.1.call-start = ((), (), s32[]{:S(2)}) async-start(), calls=%async_computation.9 | async-start | bytes 983040 | tf_op jit(solution)/shard_map/reduce_scatter | solution.py:199
Sparse Core Ops, SparseCore 0:
  11.2 109.9 all-gather.4
  124.4 135.7 all-gather.6
  263.4 77.2 all-gather.8
  343.8 77.5 all-gather.10
  446.6 18.8 reduce-scatter.1
